TPU v7x, 512 devices: a whole 4x4x16 slice. The times are simulated.
512 devices in a mesh: row: 16 (over z_lo, y), col: 32 (over z_hi, x, core).
Axes of the slice: x: 4, y: 4, z: 16 (z_hi: 4, z_lo: 4; z = z_hi * 4 + z_lo), core: 2. Of those that a mesh axis runs over, the one named last changes fastest.
Arguments:
- ancestor: float32 [20480, 20480], P('row', 'col'), as said below
- factor_rows: float32 [2, 256, 20480], P(None, 'row', 'col'), may hold values from -6 to 6
- block_lists: int32 [2, 8], replicated, may hold values from 0 to 15, as said below
Outputs:
- inverse_panel: float32 [2, 20480, 256], P(None, ('row', 'col'))
- inverse_rows: float32 [2, 256, 20480], P(None, 'col', 'row')
Inputs may be any that keep to these rules, and one draw needn't show every extreme that they name: `block_lists`: each row lists 8 distinct blocks in increasing order; the first block 0 and the last block 15 are in every row. ancestor is symmetric: ancestor[i, j] = ancestor[j, i].
All inputs are finite; a program needn't handle non-finite values.
Results may differ from a plain program's by a relative error of at most 0.000071.
Values sent between devices are 32-bit elements; how exact they have to be, the bound alone decides.
A program may use at most 64 MiB of HBM per device.

v0:
```python
import jax
import jax.numpy as jnp
from jax import lax
from jax.sharding import PartitionSpec as P

BS = 1280


def listed_mask(block_lists, blocks):
    return jnp.any(block_lists[:, :, None] == blocks[None, None, :], axis=1).astype(jnp.float32)


def per_device(ancestor, factor_rows, block_lists):
    local_rows = ancestor.shape[0]
    local_cols = ancestor.shape[1]
    col_count = lax.axis_size("col")
    row_place = lax.axis_index("row")
    col_place = lax.axis_index("col")
    col_blocks = (col_place * local_cols + lax.iota(jnp.int32, local_cols)) // BS
    masked = factor_rows * listed_mask(block_lists, col_blocks)[:, None, :]
    gathered = lax.all_gather(masked, "row", axis=1, tiled=True)
    rows_out = local_rows // col_count
    summed = lax.psum_scatter(
        -jnp.einsum(
            "ic,swc->isw",
            ancestor,
            gathered,
            precision=lax.Precision.HIGHEST,
            preferred_element_type=jnp.float32,
        ),
        "col",
        scatter_dimension=0,
        tiled=True,
    )
    first_row = (row_place * col_count + col_place) * rows_out
    row_mask = listed_mask(block_lists, (first_row + lax.iota(jnp.int32, rows_out)) // BS)
    inverse_panel = jnp.transpose(summed, (1, 0, 2)) * row_mask[:, :, None]
    arrived = lax.all_to_all(inverse_panel, "col", split_axis=2, concat_axis=1, tiled=True)
    inverse_rows = jnp.transpose(arrived, (0, 2, 1))
    return (inverse_panel, inverse_rows)


def solution(mesh):
    in_specs = (P("row", "col"), P(None, "row", "col"), P())
    out_specs = (P(None, ("row", "col"), None), P(None, "col", "row"))
    return jax.shard_map(
        per_device, mesh=mesh, in_specs=in_specs, out_specs=out_specs, check_vma=False
    )
```

profile of v0, /device:TPU:1, one launch (start us, length us, event | category | flops | bytes accessed | tf_op | source)
XLA Modules:
  0.0 525.2 jit_solution(5785872457603567026)
XLA Ops:
  7.2 0.0 copy-start
  7.2 0.0 all-gather.2.cloned.1.call-start
  7.2 0.9 compare_reduce_fusion
  8.2 1.5 broadcast_multiply_fusion
  9.7 0.0 all-gather.2.cloned.1.call-update
  9.7 0.0 all-reduce.3.cloned.1.call-start
  9.8 81.8 %all-gather.2.cloned.1.call-done = f32[2,256,640]{2,1,0:T(8,128)} async-done(((f32[2,16,640]{2,1,0:T(8,128)}), f32[2,256,640]{2,1,0:T(8,128)}) %all-gather.2.cloned.1.call-update) | async-done | bytes 1310736 | tf_op jit(solution)/shard_map/all_gather | solution.py:21
  91.6 0.0 copy-done
  91.6 9.2 %fusion.5 = f32[1280,2,256]{0,2,1:T(8,128)} fusion(f32[2,256,640]{2,1,0:T(8,128)} %all-gather.2.cloned.1.call-done, f32[1280,640]{1,0:T(8,128)S(1)} %copy-done), kind=kOutput, calls=%fused_computation.3 | convolution fusion | flops 5033820160 | bytes 7208960 | tf_op jit(solution)/shard_map/ic,swc->isw/dot_general | solution.py:24
  100.9 5.2 copy.11
  106.0 0.0 copy-start.1
  106.0 0.0 all-reduce.3.cloned.1.call-update
  106.1 0.6 copy-done.1
  106.7 0.1 compare_reduce_fusion.1
  106.8 0.1 copy.12
  106.9 1.3 dynamic-slice
  108.8 370.7 %all-reduce.3.cloned.1.call-done = f32[1280,2,256]{2,1,0:T(2,128)} async-done(((f32[1280,2,256]{2,1,0:T(2,128)}), f32[1280,2,256]{2,1,0:T(2,128)}) %all-reduce.3.cloned.1.call-update) | async-done | bytes 2621456
  479.5 1.6 fusion.8
  481.2 1.0 copy.13
  482.2 1.1 reshape.37
  483.3 14.3 %all-to-all-start = ((f32[32,1,640]{2,1,0:T(1,128)}), f32[32,1,640]{2,1,0:T(1,128)S(1)}, u32[]{:S(2)}, u32[]{:S(2)}) async-start(f32[32,1,640]{2,1,0:T(1,128)} %reshape.37), calls=%async_computation | async-start | bytes 163840 | tf_op jit(solution)/shard_map/all_to_all | solution.py:38
  497.6 1.5 copy.15
  499.1 13.2 %all-to-all-done = f32[32,1,640]{2,1,0:T(1,128)S(1)} async-done(((f32[32,1,640]{2,1,0:T(1,128)}), f32[32,1,640]{2,1,0:T(1,128)S(1)}, u32[]{:S(2)}, u32[]{:S(2)}) %all-to-all-start) | async-done | bytes 81952 | tf_op jit(solution)/shard_map/all_to_all | solution.py:38
  512.4 0.6 broadcast.51
  513.0 1.5 reduce
  514.5 1.3 reshape.38
  515.8 0.8 copy.14
  516.6 1.7 all_to_all.16
  (4 shorter events, 0.0 us)
Async XLA Ops:
  7.2 84.5 %copy-start = (f32[1280,640]{1,0:T(8,128)S(1)}, f32[1280,640]{1,0:T(8,128)}, u32[]{:S(2)}) copy-start(f32[1280,640]{1,0:T(8,128)} %param.3) | copy-start | bytes 9830404
  7.2 84.5 %all-gather.2.cloned.1.call-start = ((), (), s32[]{:S(2)}) async-start(), calls=%async_computation.1 | async-start | bytes 1392640 | tf_op jit(solution)/shard_map/all_gather | solution.py:21
  9.7 469.8 %all-reduce.3.cloned.1.call-start = ((), (), s32[]{:S(2)}) async-start(), calls=%async_computation.2 | async-start | bytes 5242880
  106.0 0.7 copy-start.1
  483.3 29.1 %all-to-all-start = ((f32[32,1,640]{2,1,0:T(1,128)}), f32[32,1,640]{2,1,0:T(1,128)S(1)}, u32[]{:S(2)}, u32[]{:S(2)}) async-start(f32[32,1,640]{2,1,0:T(1,128)} %reshape.37), calls=%async_computation | async-start | bytes 163840 | tf_op jit(solution)/shard_map/all_to_all | solution.py:38
Sparse Core Ops, SparseCore 0:
  10.6 80.9 all-gather.1
  106.2 373.3 all-reduce.2
where the time goes:
time: 526 us; the launch traced here: 525 us
  waiting for transfers between devices  466 us (89%)
  local copies, waits for them, and re-layouts  15.2 us (3%)
  between operations  14.8 us (3%)
  starting transfers between devices  14.4 us (3%)
  matrix products  9.24 us (2%)
  other arithmetic  5.73 us (1%)
    unnamed x3, waiting for transfers between devices  371 us
    all_gather x1, waiting for transfers between devices, per_device(): gathered = lax.all_gather(masked, 'row', axis=1, tiled=True)  81.8 us
    all_to_all x1, starting transfers between devices, per_device(): lax.all_to_all(inverse_panel, 'col', split_axis=2, concat_axis=1, tiled=T...  14.3 us
    all_to_all x1, waiting for transfers between devices, per_device(): lax.all_to_all(inverse_panel, 'col', split_axis=2, concat_axis=1, tiled=T...  13.2 us
  transfers between devices with their start and end apart: 3, of which 3 were waited for; matrix products, arithmetic and copies ran while one was open for 1% of the time, Pallas kernels for 0%

commit v1 on v0

v1 whole, which is shorter than its diff:
```python
import jax
import jax.numpy as jnp
from jax import lax
from jax.experimental import pallas as pl
from jax.experimental.pallas import tpu as pltpu
from jax.sharding import PartitionSpec as P

MESH = pl.DeviceIdType.MESH
F32 = jnp.float32
BF16 = jnp.bfloat16
NT = (((1,), (1,)), ((), ()))
ORDER = (2, 1, 3, 0)


def kernel(
    lists, a_hbm, f_hbm, panel, rows,
    a_v, ah, al, fbuf, fcat, ybuf, xr, zr, tin, tbuf, rbuf, pbuf,
    a_sem, ap_sem, ap_send, g_recv, g_send, x_recv, x_send, z_recv, z_send,
    t_recv, t_send, p_recv, p_send,
):
    r = lax.axis_index("row")
    c = lax.axis_index("col")
    zl, y = r // 4, r % 4
    zh, x, k = c // 8, (c // 2) % 4, c % 2
    o_k = 1 - k

    def dev(zl_, y_, zh_, x_, k_):
        return (zl_ * 4 + y_, zh_ * 8 + x_ * 2 + k_)

    partner = dev(zl, y, zh, x, o_k)
    yp, ym = (y + 1) % 4, (y + 3) % 4
    xp, xm, xo = (x + 1) % 4, (x + 3) % 4, (x + 2) % 4
    zp, zm = (zh + 1) % 4, (zh + 3) % 4

    barrier = pltpu.get_barrier_semaphore()
    near = [partner]
    for kk in range(2):
        near += [dev(zl, yp, zh, x, kk), dev(zl, ym, zh, x, kk)]
        near += [dev((zl + t) % 4, y, zh, x, kk) for t in (1, 2, 3)]
    near += [dev(zl, y, zh, xp, k), dev(zl, y, zh, xm, k)]
    near += [dev(zl, y, zp, x, k), dev(zl, y, zm, x, k)]
    for d in near:
        pl.semaphore_signal(barrier, inc=1, device_id=d, device_id_type=MESH)
    pl.semaphore_wait(barrier, len(near))

    sends = []

    def rcopy(src, dst, ssem, rsem, to, when=None):
        d = pltpu.make_async_remote_copy(
            src_ref=src, dst_ref=dst, send_sem=ssem, recv_sem=rsem,
            device_id=to, device_id_type=MESH)
        if when is None:
            d.start()
        else:
            pl.when(when)(d.start)
        sends.append((d, when))
        return d

    def got(dst, sem):
        pltpu.make_async_copy(dst, dst, sem).wait()

    kd = zl // 2
    m_src = jnp.where(kd == 0, zl, 3 - zl)
    own = (r - 8 * kd) * 16
    cols_k = pl.ds(pl.multiple_of(k * 640, 128), 640)

    def seg(kk, m):
        return jnp.where(kk == 0, m, 3 - m)

    own_rows = pl.ds(pl.multiple_of(own, 16), 16)
    g_i = [0]

    def gsem():
        g_i[0] += 1
        return g_send.at[g_i[0] - 1]

    local = []
    for s in range(2):
        dst = fbuf.at[s, own_rows, cols_k]
        sem = g_recv.at[s, r - 8 * kd, k]
        for to in (
            dev(seg(kd, 2), y, zh, x, kd),
            dev(seg(kd, 1 - m_src), y, zh, x, kd),
            dev(zl, yp, zh, x, kd),
            dev(zl, ym, zh, x, kd),
        ):
            rcopy(f_hbm.at[s], dst, gsem(), sem, to)
        rcopy(f_hbm.at[s], dst, gsem(), sem, partner, when=k != kd)
        cp = pltpu.make_async_copy(f_hbm.at[s], dst, sem)
        pl.when(k == kd)(cp.start)

    for q in range(4):
        rq = pl.ds(q * 320, 320)
        pltpu.make_async_copy(a_hbm.at[rq, :], a_v.at[rq, cols_k], a_sem.at[q]).start()
        rcopy(a_hbm.at[rq, :], a_v.at[rq, cols_k], ap_send.at[q], ap_sem.at[q], partner)

    m = seg(k, zl)
    end = dev(seg(k, 3), y, zh, x, k)

    def slot(mp, yy):
        return seg(k, mp) * 4 + yy - 8 * k

    def half(s, sl, h):
        return fbuf.at[s, pl.ds(pl.multiple_of(sl * 16, 16), 16), pl.ds(h * 640, 640)]

    def part(s, sl, h):
        return fbuf.at[s, pl.ds(pl.multiple_of(sl * 16 + h * 8, 8), 8), :]

    def gather_z(s):
        for mp in (1, 0):
            sl = slot(mp, y)
            for h in range(2):
                piece = half(s, sl, h)
                got(piece, g_recv.at[s, sl, h])
                rcopy(piece, piece, gsem(), g_recv.at[s, sl, h], end, when=m == 2)
                for yy in (yp, ym):
                    rcopy(piece, piece, gsem(), g_recv.at[s, sl, h],
                          dev(zl, yy, zh, x, k), when=m != mp)

    def gather_y(s):
        for mp in (1, 0):
            for side, (yy, to) in enumerate(((ym, yp), (yp, ym))):
                sl = slot(mp, yy)
                for h in range(2):
                    got(half(s, sl, h), g_recv.at[s, sl, h])
                piece = part(s, sl, side)
                rcopy(piece, piece, gsem(), g_recv.at[s, sl, side], dev(zl, to, zh, x, k))

    def gather_end(s):
        for mp in (1, 0):
            sl = slot(mp, (y + 2) % 4)
            for h in range(2):
                got(part(s, sl, h), g_recv.at[s, sl, h])

    cb = zh * 4 + x

    def listed(s, b):
        hit = lists[s, 0] == b
        for t in range(1, 8):
            hit = jnp.logical_or(hit, lists[s, t] == b)
        return jnp.where(hit, 1.0, 0.0).astype(F32)

    def split_a():
        for q in range(4):
            rq = pl.ds(q * 320, 320)
            got(a_v.at[rq, cols_k], a_sem.at[q])
            got(a_v.at[rq, pl.ds(pl.multiple_of(o_k * 640, 128), 640)], ap_sem.at[q])

            def step(t, _):
                at = pl.ds(pl.multiple_of(q * 320 + t * 32, 32), 32)
                v = a_v[at, :]
                hi = v.astype(BF16)
                ah[at, :] = hi
                al[at, :] = (v - hi.astype(F32)).astype(BF16)
                return 0

            lax.fori_loop(0, 10, step, 0)

    def split_f(s):
        mask = listed(s, cb)
        v = fbuf[s] * mask
        hi = v.astype(BF16)
        fcat[s, 0:128, :] = hi
        fcat[s, 128:256, :] = (v - hi.astype(F32)).astype(BF16)

    def compute(s, o):
        zc = (zh + ORDER[o]) % 4
        at = pl.ds(pl.multiple_of(zc * 320, 320), 320)
        sign = -listed(s, r)
        p1 = lax.dot_general(ah[at, :], fcat[s], NT, preferred_element_type=F32)
        p2 = lax.dot_general(al[at, :], fcat[s, 0:128, :], NT, preferred_element_type=F32)
        ybuf[s, o] = (p1[:, 0:128] + (p1[:, 128:256] + p2)) * sign

    def yp_rows(s, o, xx, h):
        return s, o, pl.ds(pl.multiple_of(xx * 80 + h * 40, 8), 40), slice(None)

    to_xp, to_xm = dev(zl, y, zh, xp, k), dev(zl, y, zh, xm, k)
    to_zp, to_zm = dev(zl, y, zp, x, k), dev(zl, y, zm, x, k)

    def xsend(s, o, kind, xx, h, to):
        rcopy(ybuf.at[yp_rows(s, o, xx, h)], xr.at[s, o, kind],
              x_send.at[s, o, kind], x_recv.at[s, o, kind], to)

    def xgot(s, o, kind):
        got(xr.at[s, o, kind], x_recv.at[s, o, kind])

    def x1(s, o):
        xsend(s, o, 0, xo, 0, to_xp)
        xsend(s, o, 1, xo, 1, to_xm)
        xsend(s, o, 4, xp, 1, to_xp)
        xsend(s, o, 5, xm, 0, to_xm)

    def x2(s, o):
        xgot(s, o, 0)
        i = yp_rows(s, o, xp, 0)
        ybuf[i] = ybuf[i] + xr[s, o, 0]
        xsend(s, o, 2, xp, 0, to_xp)
        xgot(s, o, 1)
        i = yp_rows(s, o, xm, 1)
        ybuf[i] = ybuf[i] + xr[s, o, 1]
        xsend(s, o, 3, xm, 1, to_xm)

    def x3(s, o):
        for kinds, h in (((5, 2), 0), ((4, 3), 1)):
            for kind in kinds:
                xgot(s, o, kind)
            i = yp_rows(s, o, x, h)
            ybuf[i] = ybuf[i] + xr[s, o, kinds[0]] + xr[s, o, kinds[1]]

    def zsend(s, o, kind, h, to):
        rcopy(ybuf.at[yp_rows(s, o, x, h)], zr.at[s, kind],
              z_send.at[s, kind], z_recv.at[s, kind], to)

    def zgot(s, kind):
        got(zr.at[s, kind], z_recv.at[s, kind])

    def zadd(s, o, kind, h):
        zgot(s, kind)
        i = yp_rows(s, o, x, h)
        ybuf[i] = ybuf[i] + zr[s, kind]

    def z_far(s):
        zsend(s, 0, 0, 0, to_zp)
        zsend(s, 0, 1, 1, to_zm)

    def z_direct(s, o):
        if o == 1:
            zsend(s, 1, 4, 1, to_zp)
        else:
            zsend(s, 2, 5, 0, to_zm)

    def z_sum(s, o):
        if o == 1:
            zadd(s, 1, 0, 0)
            zsend(s, 1, 2, 0, to_zp)
        else:
            zadd(s, 2, 1, 1)
            zsend(s, 2, 3, 1, to_zm)

    def finish(s):
        for kinds, h in (((5, 2), 0), ((4, 3), 1)):
            for kind in kinds:
                zgot(s, kind)
            v = ybuf[yp_rows(s, 3, x, h)] + zr[s, kinds[0]] + zr[s, kinds[1]]
            tin[s, pl.ds(h * 40, 40), :] = v
        rcopy(tin.at[s, pl.ds(pl.multiple_of(o_k * 40, 8), 40), :], pbuf.at[s],
              p_send.at[s], p_recv.at[s], partner)
        tin[s, 80:128, :] = jnp.zeros((48, 128), F32)
        tbuf[s] = tin[s].T
        for n in range(16):
            nn = (n + c) % 16
            src = tbuf.at[s, pl.ds(pl.multiple_of(nn * 8, 8), 8), :]
            dst = rbuf.at[s, cb]
            to_c = 16 * k + nn
            rcopy(src, dst, t_send.at[s, n], t_recv.at[s], (r, to_c), when=to_c != c)
            cp = pltpu.make_async_copy(src, dst, t_recv.at[s])
            pl.when(to_c == c)(cp.start)

    def outputs(s):
        panel[s, :, pl.ds(pl.multiple_of(k * 128, 128), 128)] = tin[
            s, pl.ds(pl.multiple_of(k * 40, 8), 40), :]
        got(pbuf.at[s], p_recv.at[s])
        panel[s, :, pl.ds(pl.multiple_of(o_k * 128, 128), 128)] = pbuf[s]
        got(rbuf.at[s], t_recv.at[s])
        lane = lax.broadcasted_iota(jnp.int32, (8, 128), 1)
        tiles = [jnp.zeros((8, 128), F32) for _ in range(10)]
        for n in range(16):
            t, off = (80 * n) // 128, (80 * n) % 128
            v = rbuf[s, n]
            if off:
                v = pltpu.roll(v, off, 1)
            tiles[t] = jnp.where((lane >= off) & (lane < off + 80), v, tiles[t])
            if off + 80 > 128:
                tiles[t + 1] = jnp.where(lane < off + 80 - 128, v, tiles[t + 1])
        for t in range(10):
            rows[s, :, t * 128:(t + 1) * 128] = tiles[t]

    gather_z(0)
    gather_z(1)
    split_a()
    gather_y(0)
    gather_end(0)
    split_f(0)
    compute(0, 0)
    x1(0, 0)
    compute(0, 1)
    x1(0, 1)
    gather_y(1)
    x2(0, 0)
    compute(0, 2)
    x1(0, 2)
    x2(0, 1)
    x3(0, 0)
    z_far(0)
    compute(0, 3)
    x1(0, 3)
    gather_end(1)
    split_f(1)
    compute(1, 0)
    x1(1, 0)
    x2(0, 2)
    x3(0, 1)
    z_direct(0, 1)
    x2(0, 3)
    x3(0, 2)
    z_direct(0, 2)
    compute(1, 1)
    x1(1, 1)
    z_sum(0, 1)
    z_sum(0, 2)
    x3(0, 3)
    x2(1, 0)
    compute(1, 2)
    x1(1, 2)
    x2(1, 1)
    x3(1, 0)
    z_far(1)
    compute(1, 3)
    x1(1, 3)
    x2(1, 2)
    x3(1, 1)
    z_direct(1, 1)
    x2(1, 3)
    x3(1, 2)
    z_direct(1, 2)
    finish(0)
    x3(1, 3)
    z_sum(1, 1)
    z_sum(1, 2)
    finish(1)
    outputs(0)
    outputs(1)
    for d, when in sends:
        if when is None:
            d.wait_send()
        else:
            pl.when(when)(d.wait_send)


def per_device(ancestor, factor_rows, block_lists):
    dma = pltpu.SemaphoreType.DMA
    return pl.pallas_call(
        kernel,
        out_shape=(
            jax.ShapeDtypeStruct((2, 40, 256), F32),
            jax.ShapeDtypeStruct((2, 8, 1280), F32),
        ),
        in_specs=[
            pl.BlockSpec(memory_space=pltpu.SMEM),
            pl.BlockSpec(memory_space=pl.ANY),
            pl.BlockSpec(memory_space=pl.ANY),
        ],
        out_specs=(
            pl.BlockSpec(memory_space=pltpu.VMEM),
            pl.BlockSpec(memory_space=pltpu.VMEM),
        ),
        scratch_shapes=[
            pltpu.VMEM((1280, 1280), F32),
            pltpu.VMEM((1280, 1280), BF16),
            pltpu.VMEM((1280, 1280), BF16),
            pltpu.VMEM((2, 128, 1280), F32),
            pltpu.VMEM((2, 256, 1280), BF16),
            pltpu.VMEM((2, 4, 320, 128), F32),
            pltpu.VMEM((2, 4, 6, 40, 128), F32),
            pltpu.VMEM((2, 6, 40, 128), F32),
            pltpu.VMEM((2, 128, 128), F32),
            pltpu.VMEM((2, 128, 128), F32),
            pltpu.VMEM((2, 16, 8, 128), F32),
            pltpu.VMEM((2, 40, 128), F32),
            dma((4,)),
            dma((4,)),
            dma((4,)),
            dma((2, 8, 2)),
            dma((48,)),
            dma((2, 4, 6)),
            dma((2, 4, 6)),
            dma((2, 6)),
            dma((2, 6)),
            dma((2,)),
            dma((2, 16)),
            dma((2,)),
            dma((2,)),
        ],
        compiler_params=pltpu.CompilerParams(collective_id=0, has_side_effects=True),
    )(block_lists, ancestor, factor_rows)


def solution(mesh):
    in_specs = (P("row", "col"), P(None, "row", "col"), P())
    out_specs = (P(None, ("row", "col"), None), P(None, "col", "row"))
    return jax.shard_map(
        per_device, mesh=mesh, in_specs=in_specs, out_specs=out_specs, check_vma=False
    )
```

time: 526 us -> 76 us (0.14)
  waiting for transfers between devices: 466 us -> 0 us
  Pallas kernels: 0 us -> 70.8 us
  starting transfers between devices: 14.4 us -> 0 us
  between operations: 14.8 us -> 0.64 us
  local copies, waits for them, and re-layouts: 15.2 us -> 3.05 us
  matrix products: 9.24 us -> 0 us
  other arithmetic: 5.73 us -> 0 us
    unnamed x3 -> x0, waiting for transfers between devices: 371 us -> none
    all_gather x1 -> x0, waiting for transfers between devices: 81.8 us -> none  [per_device(): gathered = lax.all_gather(masked, 'row', axis=1, tiled=True)]
    pallas_call x0 -> x1, Pallas kernels: none -> 70.8 us  [per_device(): pl.pallas_call(kernel, out_shape=(jax.ShapeDtypeStruct((2, 40, 256), F32)...]
    all_to_all x1 -> x0, starting transfers between devices: 14.3 us -> none  [per_device(): lax.all_to_all(inverse_panel, 'col', split_axis=2, concat_axis=1, tiled=T...]
    all_to_all x1 -> x0, waiting for transfers between devices: 13.2 us -> none  [per_device(): lax.all_to_all(inverse_panel, 'col', split_axis=2, concat_axis=1, tiled=T...]
    dot_general x1 -> x0, matrix products: 9.24 us -> none  [per_device(): jnp.einsum('ic,swc->isw', ancestor, gathered, precision=lax.Precision.HIG...]
  transfers between devices with their start and end apart: 3 -> 0, of which waited for: 3 -> 0; matrix products, arithmetic and copies ran while one was open for 1% -> 0% of each run, Pallas kernels for 0% -> 0%
where the time goes in v1:
time: 76 us; the launch traced here: 74.5 us
  Pallas kernels  70.8 us (93%)
  local copies, waits for them, and re-layouts  3.05 us (4%)
    pallas_call x1, Pallas kernels, per_device(): pl.pallas_call(kernel, out_shape=(jax.ShapeDtypeStruct((2, 40, 256), F32)...  70.8 us
    unnamed x2, local copies, waits for them, and re-layouts  3.05 us

profile of v1, /device:TPU:1, one launch (start us, length us, event | category | flops | bytes accessed | tf_op | source)
XLA Modules:
  0.0 74.5 jit_solution(17723034825865851700)
XLA Ops:
  0.6 70.8 %shard_map.50 = (f32[2,40,256]{2,1,0:T(8,128)}, f32[2,8,1280]{2,1,0:T(8,128)}) custom-call(s32[2,8]{1,0:T(2,128)} %lists.1, f32[1280,640]{1,0:T(8,128)} %a_hbm.1, f32[2,16,640]{2,1,0:T(8,128)} %f_hbm.1), custom_call_target="tpu_custom_call" | custom-call | tf_op jit(solution)/shard_map/pallas_call | solution.py:342
  71.4 1.5 %copy.7 = f32[2,40,256]{2,1,0:T(8,128)} copy(f32[2,40,256]{2,1,0:T(8,128)} %get-tuple-element.4) | data formatting | bytes 163840
  73.0 1.5 %copy.8 = f32[2,8,1280]{2,1,0:T(8,128)} copy(f32[2,8,1280]{2,1,0:T(8,128)} %get-tuple-element.5) | data formatting | bytes 163840

commit v2 on v1

--- a/solution.py
+++ b/solution.py
@@ -14,7 +14,7 @@
 
 def kernel(
     lists, a_hbm, f_hbm, panel, rows,
-    a_v, ah, al, fbuf, fcat, ybuf, xr, zr, tin, tbuf, rbuf, pbuf,
+    a_v, ah, al, fbuf, fcat, ybuf, xr, zr, tin, tbuf, rbuf, pbuf, ubuf,
     a_sem, ap_sem, ap_send, g_recv, g_send, x_recv, x_send, z_recv, z_send,
     t_recv, t_send, p_recv, p_send,
 ):
@@ -59,78 +59,79 @@
     def got(dst, sem):
         pltpu.make_async_copy(dst, dst, sem).wait()
 
-    kd = zl // 2
-    m_src = jnp.where(kd == 0, zl, 3 - zl)
-    own = (r - 8 * kd) * 16
     cols_k = pl.ds(pl.multiple_of(k * 640, 128), 640)
-
-    def seg(kk, m):
-        return jnp.where(kk == 0, m, 3 - m)
-
-    own_rows = pl.ds(pl.multiple_of(own, 16), 16)
+    near_z = zl + 1 - 2 * (zl % 2)
+    edge = (zl == 0) | (zl == 3)
+    others = (near_z, jnp.where(edge, (zl + 2) % 4, 3 - zl), jnp.where(edge, 3 - zl, (zl + 2) % 4))
     g_i = [0]
 
     def gsem():
         g_i[0] += 1
         return g_send.at[g_i[0] - 1]
 
-    local = []
-    for s in range(2):
-        dst = fbuf.at[s, own_rows, cols_k]
-        sem = g_recv.at[s, r - 8 * kd, k]
-        for to in (
-            dev(seg(kd, 2), y, zh, x, kd),
-            dev(seg(kd, 1 - m_src), y, zh, x, kd),
-            dev(zl, yp, zh, x, kd),
-            dev(zl, ym, zh, x, kd),
-        ):
-            rcopy(f_hbm.at[s], dst, gsem(), sem, to)
-        rcopy(f_hbm.at[s], dst, gsem(), sem, partner, when=k != kd)
-        cp = pltpu.make_async_copy(f_hbm.at[s], dst, sem)
-        pl.when(k == kd)(cp.start)
+    def shard(s, rr):
+        return fbuf.at[s, pl.ds(pl.multiple_of(rr * 8, 8), 8), :]
+
+    def half(s, rr, h):
+        return fbuf.at[s, pl.ds(pl.multiple_of(rr * 8, 8), 8), pl.ds(h * 640, 640)]
+
+    def first(s, places):
+        dst = fbuf.at[s, pl.ds(pl.multiple_of(r * 8, 8), 8), cols_k]
+        sem = g_recv.at[s, r, k]
+        for zz, yy in places:
+            for kk in range(2):
+                rcopy(f_hbm.at[s, pl.ds(kk * 8, 8), :], dst, gsem(), sem, dev(zz, yy, zh, x, kk))
+
+    def first_own(s):
+        dst = fbuf.at[s, pl.ds(pl.multiple_of(r * 8, 8), 8), cols_k]
+        sem = g_recv.at[s, r, k]
+        rcopy(f_hbm.at[s, pl.ds(pl.multiple_of(o_k * 8, 8), 8), :], dst, gsem(), sem, partner)
+        pltpu.make_async_copy(f_hbm.at[s, pl.ds(pl.multiple_of(k * 8, 8), 8), :], dst, sem).start()
+
+    def first_y(s):
+        first(s, ((zl, yp), (zl, ym)))
+
+    def first_z(s):
+        first(s, [(zz, y) for zz in others])
+
+    def forward(s, n):
+        rr = others[n] * 4 + y
+        for h in range(2):
+            got(half(s, rr, h), g_recv.at[s, rr, h])
+        for yy in (yp, ym):
+            rcopy(shard(s, rr), shard(s, rr), gsem(), g_recv.at[s, rr, 0], dev(zl, yy, zh, x, k))
+
+    def relay(s, n):
+        zz = zl if n < 0 else others[n]
+        for h, (yy, to) in enumerate(((ym, yp), (yp, ym))):
+            rr = zz * 4 + yy
+            if n < 0:
+                got(half(s, rr, 0), g_recv.at[s, rr, 0])
+                got(half(s, rr, 1), g_recv.at[s, rr, 1])
+            else:
+                got(shard(s, rr), g_recv.at[s, rr, 0])
+            piece = half(s, rr, h)
+            rcopy(piece, piece, gsem(), g_recv.at[s, rr, h], dev(zl, to, zh, x, k))
+
+    def gather_end(s):
+        for h in range(2):
+            got(half(s, r, h), g_recv.at[s, r, h])
+        for zz in (zl,) + others:
+            rr = zz * 4 + (y + 2) % 4
+            for h in range(2):
+                got(half(s, rr, h), g_recv.at[s, rr, h])
+
+    first_y(0)
+    first_z(0)
+    first_own(0)
 
     for q in range(4):
         rq = pl.ds(q * 320, 320)
         pltpu.make_async_copy(a_hbm.at[rq, :], a_v.at[rq, cols_k], a_sem.at[q]).start()
         rcopy(a_hbm.at[rq, :], a_v.at[rq, cols_k], ap_send.at[q], ap_sem.at[q], partner)
 
-    m = seg(k, zl)
-    end = dev(seg(k, 3), y, zh, x, k)
-
-    def slot(mp, yy):
-        return seg(k, mp) * 4 + yy - 8 * k
-
-    def half(s, sl, h):
-        return fbuf.at[s, pl.ds(pl.multiple_of(sl * 16, 16), 16), pl.ds(h * 640, 640)]
-
-    def part(s, sl, h):
-        return fbuf.at[s, pl.ds(pl.multiple_of(sl * 16 + h * 8, 8), 8), :]
-
-    def gather_z(s):
-        for mp in (1, 0):
-            sl = slot(mp, y)
-            for h in range(2):
-                piece = half(s, sl, h)
-                got(piece, g_recv.at[s, sl, h])
-                rcopy(piece, piece, gsem(), g_recv.at[s, sl, h], end, when=m == 2)
-                for yy in (yp, ym):
-                    rcopy(piece, piece, gsem(), g_recv.at[s, sl, h],
-                          dev(zl, yy, zh, x, k), when=m != mp)
-
-    def gather_y(s):
-        for mp in (1, 0):
-            for side, (yy, to) in enumerate(((ym, yp), (yp, ym))):
-                sl = slot(mp, yy)
-                for h in range(2):
-                    got(half(s, sl, h), g_recv.at[s, sl, h])
-                piece = part(s, sl, side)
-                rcopy(piece, piece, gsem(), g_recv.at[s, sl, side], dev(zl, to, zh, x, k))
-
-    def gather_end(s):
-        for mp in (1, 0):
-            sl = slot(mp, (y + 2) % 4)
-            for h in range(2):
-                got(part(s, sl, h), g_recv.at[s, sl, h])
+    first_z(1)
+    first_own(1)
 
     cb = zh * 4 + x
 
@@ -140,21 +141,20 @@
             hit = jnp.logical_or(hit, lists[s, t] == b)
         return jnp.where(hit, 1.0, 0.0).astype(F32)
 
-    def split_a():
-        for q in range(4):
-            rq = pl.ds(q * 320, 320)
-            got(a_v.at[rq, cols_k], a_sem.at[q])
-            got(a_v.at[rq, pl.ds(pl.multiple_of(o_k * 640, 128), 640)], ap_sem.at[q])
-
-            def step(t, _):
-                at = pl.ds(pl.multiple_of(q * 320 + t * 32, 32), 32)
-                v = a_v[at, :]
-                hi = v.astype(BF16)
-                ah[at, :] = hi
-                al[at, :] = (v - hi.astype(F32)).astype(BF16)
-                return 0
-
-            lax.fori_loop(0, 10, step, 0)
+    def split_a(q):
+        rq = pl.ds(q * 320, 320)
+        got(a_v.at[rq, cols_k], a_sem.at[q])
+        got(a_v.at[rq, pl.ds(pl.multiple_of(o_k * 640, 128), 640)], ap_sem.at[q])
+
+        def step(t, _):
+            at = pl.ds(pl.multiple_of(q * 320 + t * 32, 32), 32)
+            v = a_v[at, :]
+            hi = v.astype(BF16)
+            ah[at, :] = hi
+            al[at, :] = (v - hi.astype(F32)).astype(BF16)
+            return 0
+
+        lax.fori_loop(0, 10, step, 0)
 
     def split_f(s):
         mask = listed(s, cb)
@@ -248,19 +248,21 @@
         tin[s, 80:128, :] = jnp.zeros((48, 128), F32)
         tbuf[s] = tin[s].T
         for n in range(16):
-            nn = (n + c) % 16
+            nn = (n + cb) % 16
             src = tbuf.at[s, pl.ds(pl.multiple_of(nn * 8, 8), 8), :]
             dst = rbuf.at[s, cb]
-            to_c = 16 * k + nn
-            rcopy(src, dst, t_send.at[s, n], t_recv.at[s], (r, to_c), when=to_c != c)
-            cp = pltpu.make_async_copy(src, dst, t_recv.at[s])
-            pl.when(to_c == c)(cp.start)
+            if n:
+                rcopy(src, dst, t_send.at[s, n], t_recv.at[s], (r, 2 * nn + k))
+            else:
+                pltpu.make_async_copy(src, dst, t_recv.at[s]).start()
 
     def outputs(s):
-        panel[s, :, pl.ds(pl.multiple_of(k * 128, 128), 128)] = tin[
-            s, pl.ds(pl.multiple_of(k * 40, 8), 40), :]
         got(pbuf.at[s], p_recv.at[s])
-        panel[s, :, pl.ds(pl.multiple_of(o_k * 128, 128), 128)] = pbuf[s]
+        both = jnp.concatenate([
+            tin[s, pl.ds(pl.multiple_of(k * 40, 8), 40), :], pbuf[s], jnp.zeros((48, 128), F32)], axis=0).T
+        ubuf[s, :, k] = both.reshape(16, 8, 128)
+        ubuf[s, :, o_k] = pltpu.roll(both, 88, 1).reshape(16, 8, 128)
+        panel[s] = ubuf[s].reshape(256, 128).T[0:40, :]
         got(rbuf.at[s], t_recv.at[s])
         lane = lax.broadcasted_iota(jnp.int32, (8, 128), 1)
         tiles = [jnp.zeros((8, 128), F32) for _ in range(10)]
@@ -275,60 +277,69 @@
         for t in range(10):
             rows[s, :, t * 128:(t + 1) * 128] = tiles[t]
 
-    gather_z(0)
-    gather_z(1)
-    split_a()
-    gather_y(0)
+    forward(0, 0)
+    split_a(0)
+    relay(0, -1)
+    forward(0, 1)
+    split_a(1)
+    relay(0, 0)
+    forward(0, 2)
+    split_a(2)
+    relay(0, 1)
+    first_y(1)
+    forward(1, 0)
+    split_a(3)
+    relay(0, 2)
+    forward(1, 1)
+    relay(1, -1)
+    forward(1, 2)
     gather_end(0)
     split_f(0)
-    compute(0, 0)
-    x1(0, 0)
-    compute(0, 1)
-    x1(0, 1)
-    gather_y(1)
+    for o in range(4):
+        compute(0, o)
+        x1(0, o)
+        relay(1, 0) if o == 1 else None
+    relay(1, 1)
     x2(0, 0)
-    compute(0, 2)
-    x1(0, 2)
     x2(0, 1)
+    relay(1, 2)
+    x2(0, 2)
+    x2(0, 3)
     x3(0, 0)
     z_far(0)
-    compute(0, 3)
-    x1(0, 3)
+    x3(0, 1)
+    z_direct(0, 1)
     gather_end(1)
     split_f(1)
     compute(1, 0)
     x1(1, 0)
-    x2(0, 2)
-    x3(0, 1)
-    z_direct(0, 1)
-    x2(0, 3)
+    compute(1, 1)
+    x1(1, 1)
     x3(0, 2)
     z_direct(0, 2)
-    compute(1, 1)
-    x1(1, 1)
-    z_sum(0, 1)
-    z_sum(0, 2)
+    compute(1, 2)
+    x1(1, 2)
+    compute(1, 3)
+    x1(1, 3)
     x3(0, 3)
     x2(1, 0)
-    compute(1, 2)
-    x1(1, 2)
     x2(1, 1)
+    z_sum(0, 1)
+    x2(1, 2)
+    x2(1, 3)
+    z_sum(0, 2)
     x3(1, 0)
     z_far(1)
-    compute(1, 3)
-    x1(1, 3)
-    x2(1, 2)
     x3(1, 1)
     z_direct(1, 1)
-    x2(1, 3)
     x3(1, 2)
     z_direct(1, 2)
+    x3(1, 3)
     finish(0)
-    x3(1, 3)
     z_sum(1, 1)
     z_sum(1, 2)
+    outputs(0)
     finish(1)
-    outputs(0)
     outputs(1)
     for d, when in sends:
         if when is None:
@@ -367,11 +378,12 @@
             pltpu.VMEM((2, 128, 128), F32),
             pltpu.VMEM((2, 16, 8, 128), F32),
             pltpu.VMEM((2, 40, 128), F32),
+            pltpu.VMEM((2, 16, 2, 8, 128), F32),
             dma((4,)),
             dma((4,)),
             dma((4,)),
-            dma((2, 8, 2)),
-            dma((48,)),
+            dma((2, 16, 2)),
+            dma((50,)),
             dma((2, 4, 6)),
             dma((2, 4, 6)),
             dma((2, 6)),

time: 76 us -> 77.5 us (1.020)
  the two profiles are of different devices: /device:TPU:1 before, /device:TPU:6 now
where the time goes in v2:
time: 77.5 us; the launch traced here: 77.3 us
  Pallas kernels  73.6 us (95%)
  local copies, waits for them, and re-layouts  3.05 us (4%)
    pallas_call x1, Pallas kernels, per_device(): pl.pallas_call(kernel, out_shape=(jax.ShapeDtypeStruct((2, 40, 256), F32)...  73.6 us
    unnamed x2, local copies, waits for them, and re-layouts  3.05 us

profile of v2, /device:TPU:6, one launch (start us, length us, event | category | flops | bytes accessed | tf_op | source)
XLA Modules:
  0.0 77.3 jit_solution(7564788852990343651)
XLA Ops:
  0.6 73.6 %shard_map.50 = (f32[2,40,256]{2,1,0:T(8,128)}, f32[2,8,1280]{2,1,0:T(8,128)}) custom-call(s32[2,8]{1,0:T(2,128)} %lists.1, f32[1280,640]{1,0:T(8,128)} %a_hbm.1, f32[2,16,640]{2,1,0:T(8,128)} %f_hbm.1), custom_call_target="tpu_custom_call" | custom-call | tf_op jit(solution)/shard_map/pallas_call | solution.py:353
  74.2 1.5 %copy.7 = f32[2,40,256]{2,1,0:T(8,128)} copy(f32[2,40,256]{2,1,0:T(8,128)} %get-tuple-element.4) | data formatting | bytes 163840
  75.8 1.5 %copy.8 = f32[2,8,1280]{2,1,0:T(8,128)} copy(f32[2,8,1280]{2,1,0:T(8,128)} %get-tuple-element.5) | data formatting | bytes 163840

commit v3 on v2

--- a/solution.py
+++ b/solution.py
@@ -16,7 +16,7 @@
     lists, a_hbm, f_hbm, panel, rows,
     a_v, ah, al, fbuf, fcat, ybuf, xr, zr, tin, tbuf, rbuf, pbuf, ubuf,
     a_sem, ap_sem, ap_send, g_recv, g_send, x_recv, x_send, z_recv, z_send,
-    t_recv, t_send, p_recv, p_send,
+    t_recv, t_send, p_recv, p_send, ready,
 ):
     r = lax.axis_index("row")
     c = lax.axis_index("col")
@@ -32,17 +32,31 @@
     xp, xm, xo = (x + 1) % 4, (x + 3) % 4, (x + 2) % 4
     zp, zm = (zh + 1) % 4, (zh + 3) % 4
 
+    z = zh * 4 + zl
+
+    def zdev(t, kk):
+        zz = (z + t) % 16
+        return dev(zz % 4, y, zz // 4, x, kk)
+
     barrier = pltpu.get_barrier_semaphore()
     near = [partner]
     for kk in range(2):
         near += [dev(zl, yp, zh, x, kk), dev(zl, ym, zh, x, kk)]
-        near += [dev((zl + t) % 4, y, zh, x, kk) for t in (1, 2, 3)]
+        near += [zdev(1, kk), zdev(15, kk)]
     near += [dev(zl, y, zh, xp, k), dev(zl, y, zh, xm, k)]
-    near += [dev(zl, y, zp, x, k), dev(zl, y, zm, x, k)]
     for d in near:
         pl.semaphore_signal(barrier, inc=1, device_id=d, device_id_type=MESH)
     pl.semaphore_wait(barrier, len(near))
 
+    def tell(stage):
+        pl.semaphore_signal(ready.at[0, stage], inc=1, device_id=zdev(1, k), device_id_type=MESH)
+        pl.semaphore_signal(ready.at[1, stage], inc=1, device_id=zdev(15, k), device_id_type=MESH)
+
+    def heard(stage):
+        pl.semaphore_wait(ready.at[0, stage], 1)
+        pl.semaphore_wait(ready.at[1, stage], 1)
+
+    tell(0)
     sends = []
 
     def rcopy(src, dst, ssem, rsem, to, when=None):
@@ -92,12 +106,26 @@
         first(s, ((zl, yp), (zl, ym)))
 
     def first_z(s):
-        first(s, [(zz, y) for zz in others])
-
-    def forward(s, n):
+        dst = fbuf.at[s, pl.ds(pl.multiple_of(r * 8, 8), 8), cols_k]
+        sem = g_recv.at[s, r, k]
+        for zz, ok in ((zl + 1, zl < 3), (zl - 1, zl > 0)):
+            for kk in range(2):
+                rcopy(f_hbm.at[s, pl.ds(kk * 8, 8), :], dst, gsem(), sem,
+                      dev(zz, y, zh, x, kk), when=ok)
+
+    def onward(s, n):
         rr = others[n] * 4 + y
         for h in range(2):
-            got(half(s, rr, h), g_recv.at[s, rr, h])
+            piece = half(s, rr, h)
+            sem = g_recv.at[s, rr, h]
+            got(piece, sem)
+            rcopy(piece, piece, gsem(), sem, dev(zl + 1, y, zh, x, k),
+                  when=(others[n] < zl) & (zl < 3))
+            rcopy(piece, piece, gsem(), sem, dev(zl - 1, y, zh, x, k),
+                  when=(others[n] > zl) & (zl > 0))
+
+    def spread(s, n):
+        rr = others[n] * 4 + y
         for yy in (yp, ym):
             rcopy(shard(s, rr), shard(s, rr), gsem(), g_recv.at[s, rr, 0], dev(zl, yy, zh, x, k))
 
@@ -121,8 +149,10 @@
             for h in range(2):
                 got(half(s, rr, h), g_recv.at[s, rr, h])
 
+    first_z(0)
     first_y(0)
-    first_z(0)
+    first_z(1)
+    first_y(1)
     first_own(0)
 
     for q in range(4):
@@ -130,7 +160,6 @@
         pltpu.make_async_copy(a_hbm.at[rq, :], a_v.at[rq, cols_k], a_sem.at[q]).start()
         rcopy(a_hbm.at[rq, :], a_v.at[rq, cols_k], ap_send.at[q], ap_sem.at[q], partner)
 
-    first_z(1)
     first_own(1)
 
     cb = zh * 4 + x
@@ -277,50 +306,65 @@
         for t in range(10):
             rows[s, :, t * 128:(t + 1) * 128] = tiles[t]
 
-    forward(0, 0)
+    onward(0, 0)
+    spread(0, 0)
+    onward(1, 0)
+    spread(1, 0)
+    heard(0)
+    tell(1)
     split_a(0)
+    onward(0, 1)
+    spread(0, 1)
+    onward(1, 1)
+    spread(1, 1)
+    heard(1)
+    tell(2)
+    split_a(1)
+    onward(0, 2)
+    spread(0, 2)
+    onward(1, 2)
+    spread(1, 2)
+    heard(2)
     relay(0, -1)
-    forward(0, 1)
-    split_a(1)
+    relay(1, -1)
+    split_a(2)
     relay(0, 0)
-    forward(0, 2)
-    split_a(2)
+    relay(1, 0)
+    split_a(3)
     relay(0, 1)
-    first_y(1)
-    forward(1, 0)
-    split_a(3)
+    relay(1, 1)
     relay(0, 2)
-    forward(1, 1)
-    relay(1, -1)
-    forward(1, 2)
+    relay(1, 2)
     gather_end(0)
     split_f(0)
-    for o in range(4):
-        compute(0, o)
-        x1(0, o)
-        relay(1, 0) if o == 1 else None
-    relay(1, 1)
+    compute(0, 0)
+    x1(0, 0)
+    compute(0, 1)
+    x1(0, 1)
+    compute(0, 2)
+    x1(0, 2)
+    compute(0, 3)
+    x1(0, 3)
+    gather_end(1)
+    split_f(1)
     x2(0, 0)
+    compute(1, 0)
+    x1(1, 0)
     x2(0, 1)
-    relay(1, 2)
+    compute(1, 1)
+    x1(1, 1)
     x2(0, 2)
     x2(0, 3)
     x3(0, 0)
     z_far(0)
+    compute(1, 2)
+    x1(1, 2)
     x3(0, 1)
     z_direct(0, 1)
-    gather_end(1)
-    split_f(1)
-    compute(1, 0)
-    x1(1, 0)
-    compute(1, 1)
-    x1(1, 1)
+    compute(1, 3)
+    x1(1, 3)
     x3(0, 2)
     z_direct(0, 2)
-    compute(1, 2)
-    x1(1, 2)
-    compute(1, 3)
-    x1(1, 3)
     x3(0, 3)
     x2(1, 0)
     x2(1, 1)
@@ -338,8 +382,8 @@
     finish(0)
     z_sum(1, 1)
     z_sum(1, 2)
+    finish(1)
     outputs(0)
-    finish(1)
     outputs(1)
     for d, when in sends:
         if when is None:
@@ -358,8 +402,8 @@
         ),
         in_specs=[
             pl.BlockSpec(memory_space=pltpu.SMEM),
-            pl.BlockSpec(memory_space=pl.ANY),
-            pl.BlockSpec(memory_space=pl.ANY),
+            pl.BlockSpec(memory_space=pltpu.HBM),
+            pl.BlockSpec(memory_space=pltpu.HBM),
         ],
         out_specs=(
             pl.BlockSpec(memory_space=pltpu.VMEM),
@@ -383,7 +427,7 @@
             dma((4,)),
             dma((4,)),
             dma((2, 16, 2)),
-            dma((50,)),
+            dma((70,)),
             dma((2, 4, 6)),
             dma((2, 4, 6)),
             dma((2, 6)),
@@ -392,8 +436,9 @@
             dma((2, 16)),
             dma((2,)),
             dma((2,)),
+            pltpu.SemaphoreType.REGULAR((2, 3)),
         ],
-        compiler_params=pltpu.CompilerParams(collective_id=0, has_side_effects=True),
+        compiler_params=pltpu.CompilerParams(collective_id=0, has_side_effects=True, vmem_limit_bytes=26 * 1024 * 1024),
     )(block_lists, ancestor, factor_rows)
 
 

time: 77.5 us -> 74.6 us (0.963)
  the two profiles are of different devices: /device:TPU:6 before, /device:TPU:8 now
where the time goes in v3:
time: 74.6 us; the launch traced here: 74.4 us
  Pallas kernels  69 us (92%)
  local copies, waits for them, and re-layouts  4.76 us (6%)
    pallas_call x1, Pallas kernels, per_device(): pl.pallas_call(kernel, out_shape=(jax.ShapeDtypeStruct((2, 40, 256), F32)...  69 us
    unnamed x8, local copies, waits for them, and re-layouts  4.76 us

profile of v3, /device:TPU:8, one launch (start us, length us, event | category | flops | bytes accessed | tf_op | source)
XLA Modules:
  0.0 74.4 jit_solution(13938840795734491572)
XLA Ops:
  0.6 0.0 copy-start
  0.6 1.9 %copy-done = f32[1280,640]{1,0:T(8,128)S(1)} copy-done((f32[1280,640]{1,0:T(8,128)S(1)}, f32[1280,640]{1,0:T(8,128)}, u32[]{:S(2)}) %copy-start) | copy-done | bytes 3276824
  2.6 0.0 copy-start.1
  2.6 0.9 %copy-done.1 = f32[2,16,640]{2,1,0:T(8,128)S(1)} copy-done((f32[2,16,640]{2,1,0:T(8,128)S(1)}, f32[2,16,640]{2,1,0:T(8,128)}, u32[]{:S(2)}) %copy-start.1) | copy-done | bytes 81944
  3.4 0.0 copy-start.2
  3.4 0.7 copy-done.2
  4.1 69.0 %shard_map.50 = (f32[2,40,256]{2,1,0:T(8,128)S(1)}, f32[2,8,1280]{2,1,0:T(8,128)S(1)}) custom-call(s32[2,8]{1,0:T(2,128)S(1)} %copy-done.2, f32[1280,640]{1,0:T(8,128)S(1)} %copy-done, f32[2,16,640]{2,1,0:T(8,128)S(1)} %copy-done.1), custom_call_target="tpu_custom_call" | custom-call | tf_op jit(solution)/shard_map/pallas_call | solution.py:397
  73.1 0.6 copy.7
  73.7 0.6 copy.8
Async XLA Ops:
  0.6 1.9 %copy-start = (f32[1280,640]{1,0:T(8,128)S(1)}, f32[1280,640]{1,0:T(8,128)}, u32[]{:S(2)}) copy-start(f32[1280,640]{1,0:T(8,128)} %a_hbm.1) | copy-start | bytes 9830404
  2.6 0.9 %copy-start.1 = (f32[2,16,640]{2,1,0:T(8,128)S(1)}, f32[2,16,640]{2,1,0:T(8,128)}, u32[]{:S(2)}) copy-start(f32[2,16,640]{2,1,0:T(8,128)} %f_hbm.1) | copy-start | bytes 245764
  3.4 0.7 copy-start.2
